TPU v7x, 512 devices: a whole 4x4x16 slice. The times are simulated.
512 devices in a mesh: rep: 64 (over x_lo, z, core), tp: 8 (over y, x_hi).
Axes of the slice: x: 4 (x_hi: 2, x_lo: 2; x = x_hi * 2 + x_lo), y: 4, z: 16, core: 2. Of those that a mesh axis runs over, the one named last changes fastest.
Arguments:
- prompt_q: bfloat16 [32768, 2048], P('rep', 'tp'), may hold values from -24 to 24
- prompt_k: bfloat16 [32768, 2048], P('rep', 'tp'), may hold values from -24 to 24
- prompt_v: bfloat16 [32768, 2048], P('rep', 'tp'), may hold values from -6 to 6
- prompt_len: int32 [64], P('rep'), may hold values from 256 to 512, as said below
- cache_keys: bfloat16 [128, 1024, 2048], P('rep', None, 'tp'), may hold values from -24 to 24
- cache_values: bfloat16 [128, 1024, 2048], P('rep', None, 'tp'), may hold values from -6 to 6
- new_q: bfloat16 [128, 2048], P('rep', 'tp'), may hold values from -24 to 24
- new_k: bfloat16 [128, 2048], P('rep', 'tp'), may hold values from -6 to 6
- new_v: bfloat16 [128, 2048], P('rep', 'tp'), may hold values from -6 to 6
- cache_len: int32 [128], replicated, may hold values from 260 to 1024, as said below
- moving: int32 [64], replicated, may hold values from 0 to 1
- out_weight: bfloat16 [2048, 2048], P(None, 'tp'), may hold values from -0.125 to 0.125
- out_bias: float32 [2048], P('tp'), may hold values from -1.75 to 1.75
- residual: bfloat16 [32896, 2048], P('rep', 'tp'), may hold values from -150 to 150
- ln_gain: float32 [2048], P('tp'), may hold values from 0.1 to 1.9
- ln_shift: float32 [2048], P('tp'), may hold values from -1.75 to 1.75
Outputs:
- hidden_out: bfloat16 [32896, 2048], P('rep', 'tp')
- normed: bfloat16 [32896, 2048], P('rep', 'tp')
- moved_window: bfloat16 [64, 2, 260, 2048], P('rep', None, None, 'tp')
Inputs may be any that keep to these rules, and one draw needn't show every extreme that they name: `prompt_len`: some replica's prompt has all 512 tokens live. `cache_len`: some request's cache is full.
All inputs are finite; a program needn't handle non-finite values.
Results may differ from a plain program's by a relative error of at most 0.0022.
Values may be sent and summed in bfloat16 or wider, within the bound.
No kernel may reach another device: no remote copies, remote signals or barrier semaphores. Data moves between devices by JAX's collectives and lax.ppermute only.
A program may use at most 64 MiB of HBM per device.

v0:
```python
import math
import jax
import jax.numpy as jnp
from jax import lax
from jax.sharding import PartitionSpec as P

D = 2048
HEADS = 16
HD = 128
SINK = 4
WIN = 256
masked_score = -1e30
norm_epsilon = 1e-05


def from_behind(block, axis, distance):
    devices = range(lax.axis_size(axis))
    route = [((i - distance) % len(devices), i) for i in devices]
    return lax.ppermute(block, axis, route)


def head_slopes(local_heads):
    first_head = lax.axis_index("tp") * local_heads
    head_ids = (first_head + jnp.arange(local_heads, dtype=jnp.int32)).astype(jnp.float32)
    return jnp.exp2(-8.0 * (head_ids + 1.0) / HEADS)


def softmax_rows(scores):
    row_max = jnp.max(scores, axis=-1, keepdims=True)
    expo_terms = jnp.exp(scores - row_max)
    return (expo_terms / jnp.sum(expo_terms, axis=-1, keepdims=True)).astype(jnp.bfloat16)


def prompt_attend(query_rows, key_rows, value_rows, length, slopes):
    row_count = query_rows.shape[0]
    local_heads = slopes.shape[0]
    query_heads = query_rows.reshape(row_count, local_heads, HD)
    key_heads = key_rows.reshape(row_count, local_heads, HD)
    value_heads = value_rows.reshape(row_count, local_heads, HD)
    scores = jnp.einsum(
        "qhd,khd->hqk", query_heads, key_heads, preferred_element_type=jnp.float32
    ) * (1.0 / math.sqrt(HD))
    position = jnp.arange(row_count, dtype=jnp.int32)
    distance = (position[:, None] - position[None, :]).astype(jnp.float32)
    scores = scores - slopes[:, None, None] * distance[None]
    allowed = (position[None, :] <= position[:, None]) & (position[None, :] < length)
    scores = jnp.where(allowed[None], scores, masked_score)
    weights = softmax_rows(scores)
    mixed_heads = jnp.einsum(
        "hqk,khd->qhd", weights, value_heads, preferred_element_type=jnp.float32
    )
    return mixed_heads.astype(jnp.bfloat16).reshape(row_count, local_heads * HD)


def window_rows(cache_rows, newest, length):
    middle = lax.dynamic_slice_in_dim(cache_rows, length + 1 - WIN, WIN - 1, 0)
    return jnp.concatenate([cache_rows[:SINK], middle, newest[None]], axis=0)


def window_positions(length):
    sink_part = jnp.arange(SINK, dtype=jnp.int32)
    tail_part = length + 1 - WIN + jnp.arange(WIN, dtype=jnp.int32)
    return jnp.concatenate([sink_part, tail_part])


def decode_attend(query_row, key_window, value_window, length, slopes):
    local_heads = slopes.shape[0]
    query_heads = query_row.reshape(local_heads, HD)
    key_heads = key_window.reshape(-1, local_heads, HD)
    value_heads = value_window.reshape(-1, local_heads, HD)
    scores = jnp.einsum(
        "hd,whd->hw", query_heads, key_heads, preferred_element_type=jnp.float32
    ) * (1.0 / math.sqrt(HD))
    distance = (length - window_positions(length)).astype(jnp.float32)
    scores = scores - slopes[:, None] * distance[None, :]
    weights = softmax_rows(scores)
    mixed_heads = jnp.einsum("hw,whd->hd", weights, value_heads, preferred_element_type=jnp.float32)
    return mixed_heads.astype(jnp.bfloat16).reshape(local_heads * HD)


def select_slot(stacked, slot_index):
    return lax.dynamic_index_in_dim(stacked, slot_index, 0, keepdims=False)


def on_device(
    prompt_q,
    prompt_k,
    prompt_v,
    prompt_len,
    cache_keys,
    cache_values,
    new_q,
    new_k,
    new_v,
    cache_len,
    moving,
    out_weight,
    out_bias,
    residual,
    ln_gain,
    ln_shift,
):
    replica_count = lax.axis_size("rep")
    replica_index = lax.axis_index("rep")
    partner = (replica_index + replica_count // 2) % replica_count
    local_heads = prompt_q.shape[1] // HD
    slopes = head_slopes(local_heads)
    prompt_mix = prompt_attend(prompt_q, prompt_k, prompt_v, prompt_len[0], slopes)
    slot_count = cache_keys.shape[0]
    leaving = moving[replica_index]
    staying = 1 - leaving
    stay_len = cache_len[replica_index * slot_count + staying]
    come_len = cache_len[partner * slot_count + moving[partner]]
    stay_keys = window_rows(select_slot(cache_keys, staying), select_slot(new_k, staying), stay_len)
    stay_values = window_rows(
        select_slot(cache_values, staying), select_slot(new_v, staying), stay_len
    )
    stay_out = decode_attend(select_slot(new_q, staying), stay_keys, stay_values, stay_len, slopes)
    come_cache_keys, come_cache_values, come_query, come_key, come_value = from_behind(
        (
            select_slot(cache_keys, leaving),
            select_slot(cache_values, leaving),
            select_slot(new_q, leaving),
            select_slot(new_k, leaving),
            select_slot(new_v, leaving),
        ),
        "rep",
        replica_count // 2,
    )
    come_keys = window_rows(come_cache_keys, come_key, come_len)
    come_values = window_rows(come_cache_values, come_value, come_len)
    come_out = decode_attend(come_query, come_keys, come_values, come_len, slopes)
    mixed_rows = jnp.concatenate([prompt_mix, stay_out[None], come_out[None]], axis=0)
    projected = jnp.dot(
        lax.all_gather(mixed_rows, "tp", axis=1, tiled=True),
        out_weight,
        preferred_element_type=jnp.float32,
    )
    stream = projected + out_bias[None, :] + residual.astype(jnp.float32)
    hidden_out = stream.astype(jnp.bfloat16)
    row_total = jnp.sum(stream, axis=1)
    row_mean = lax.psum(row_total, "tp") / D
    centered = stream - row_mean[:, None]
    row_var = lax.psum(jnp.sum(centered * centered, axis=1), "tp") / D
    normed = (
        centered * lax.rsqrt(row_var + norm_epsilon)[:, None] * ln_gain[None, :] + ln_shift[None, :]
    ).astype(jnp.bfloat16)
    moved_window = jnp.stack([come_keys, come_values], axis=0)[None]
    return (hidden_out, normed, moved_window)


def solution(mesh):
    in_specs = (
        P("rep", "tp"),
        P("rep", "tp"),
        P("rep", "tp"),
        P("rep"),
        P("rep", None, "tp"),
        P("rep", None, "tp"),
        P("rep", "tp"),
        P("rep", "tp"),
        P("rep", "tp"),
        P(),
        P(),
        P(None, "tp"),
        P("tp"),
        P("rep", "tp"),
        P("tp"),
        P("tp"),
    )
    out_specs = (P("rep", "tp"), P("rep", "tp"), P("rep", None, None, "tp"))
    return jax.shard_map(
        on_device, mesh=mesh, in_specs=in_specs, out_specs=out_specs, check_vma=False
    )
```

profile of v0, /device:TPU:32, one launch (start us, length us, event | category | flops | bytes accessed | tf_op | source)
XLA Modules:
  0.0 192.9 jit_solution(14140378695549050792)
XLA Ops:
  7.3 1.3 fusion.47
  10.6 1.1 dynamic-slice_bitcast_fusion.1
  11.6 3.4 %collective-permute-start.1 = (bf16[1024,256]{1,0:T(8,128)(2,1)S(1)}, bf16[1024,256]{1,0:T(8,128)(2,1)}, u32[]{:S(2)}, u32[]{:S(2)}) collective-permute-start(bf16[1024,256]{1,0:T(8,128)(2,1)S(1)} %dynamic-slice_bitcast_fusion.1), channel_id=1, source_target_pairs={{256,0},{264,8},{272,16},{280,24},{288,32},{296,40},{304,48},{312,... | collective-permute-start | bytes 1572872 | tf_op jit(solution)/shard_map/ppermute | solution.py:19
  16.3 1.4 fusion.33
  17.7 2.4 %collective-permute-start.2 = (bf16[256]{0:T(256)(128)(2,1)}, bf16[256]{0:T(256)(128)(2,1)}, u32[]{:S(2)}, u32[]{:S(2)}) collective-permute-start(bf16[256]{0:T(256)(128)(2,1)} %get-tuple-element.10), channel_id=1, source_target_pairs={{256,0},{264,8},{272,16},{280,24},{288,32},{296,40},{304,48},{312,... | collective-permute-start | bytes 1544 | tf_op jit(solution)/shard_map/ppermute | solution.py:19
  20.2 1.2 fusion.35
  21.4 3.4 %collective-permute-start = (bf16[256]{0:T(256)(128)(2,1)}, bf16[256]{0:T(256)(128)(2,1)}, u32[]{:S(2)}, u32[]{:S(2)}) collective-permute-start(bf16[256]{0:T(256)(128)(2,1)} %fusion.35), channel_id=1, source_target_pairs={{256,0},{264,8},{272,16},{280,24},{288,32},{296,40},{304,48},{312,... | collective-permute-start | bytes 1544 | tf_op jit(solution)/shard_map/ppermute | solution.py:19
  24.8 1.1 dynamic-slice_bitcast_fusion
  25.9 2.4 %collective-permute-start.3 = (bf16[1024,256]{1,0:T(8,128)(2,1)S(1)}, bf16[1024,256]{1,0:T(8,128)(2,1)}, u32[]{:S(2)}, u32[]{:S(2)}) collective-permute-start(bf16[1024,256]{1,0:T(8,128)(2,1)S(1)} %dynamic-slice_bitcast_fusion), channel_id=1, source_target_pairs={{256,0},{264,8},{272,16},{280,24},{288,32},{296,40},{304,48},{312,... | collective-permute-start | bytes 1572872 | tf_op jit(solution)/shard_map/ppermute | solution.py:19
  28.3 0.6 fusion.34
  28.9 3.4 %collective-permute-start.4 = (bf16[256]{0:T(256)(128)(2,1)}, bf16[256]{0:T(256)(128)(2,1)}, u32[]{:S(2)}, u32[]{:S(2)}) collective-permute-start(bf16[256]{0:T(256)(128)(2,1)} %get-tuple-element.12), channel_id=1, source_target_pairs={{256,0},{264,8},{272,16},{280,24},{288,32},{296,40},{304,48},{312,... | collective-permute-start | bytes 1544 | tf_op jit(solution)/shard_map/ppermute | solution.py:19
  33.0 0.6 fusion.46
  36.0 0.7 constant_dynamic-slice_fusion.10
  36.7 0.6 iota_add_fusion
  37.3 0.7 constant_dynamic-slice_fusion.7
  38.1 1.0 constant_dynamic-slice_fusion.6
  39.3 0.2 pad_maximum_fusion.1
  39.5 0.1 fusion.13
  39.7 0.6 multiply_exponential_fusion
  41.1 0.1 fusion.2
  41.2 1.8 copy.50
  43.0 2.0 %fusion.24 = (f32[260]{0:T(512)S(1)}, f32[260]{0:T(512)S(1)}) fusion(s32[4]{0:T(128)S(1)} %iota.55, s32[256]{0:T(256)} %get-tuple-element.30, s32[]{:T(128)} %bitcast.6, s32[256]{0:T(256)} %get-tuple-element.29, s32[]{:T(128)} %bitcast.15), kind=kLoop, calls=%fused_computation.60 | loop fusion | flops 1560 | bytes 4152 | tf_op jit(solution)/shard_map/convert_element_type | solution.py:74
  45.0 1.5 pad_maximum_fusion.2
  46.5 3.0 %subtract_select_fusion = f32[2,512,512]{1,2,0:T(8,128)} fusion(f32[512,512]{0,1:T(8,128)S(1)} %subtract_convert_fusion, f32[2]{0:T(128)} %multiply_exponential_fusion, pred[512,512]{0,1:T(8,128)(4,1)S(1)} %fusion.2, bf16[512,256]{1,0:T(8,128)(2,1)} %param.17, bf16[512,256]{1,0:T(8,128)(2,1)} %param.16), kind=kOutput, calls=%fused_computation.3 | convolution fusion | flops 136314880 | bytes 3932168 | tf_op jit(solution)/shard_map/qhd,khd->hqk/dot_general | solution.py:40
  49.5 2.0 %fusion.48 = f32[2,512]{1,0:T(2,128)S(1)} fusion(f32[512,512]{0,1:T(8,128)S(1)} %subtract_convert_fusion, f32[2]{0:T(128)S(1)} %copy-done.4, pred[512,512]{0,1:T(8,128)(4,1)S(1)} %fusion.2, bf16[512,256]{1,0:T(8,128)(2,1)} %param.17, bf16[512,256]{1,0:T(8,128)(2,1)} %param.16), kind=kOutput, calls=%fused_computation.90 | convolution fusion | flops 137363968 | bytes 1839112 | tf_op jit(solution)/shard_map/sub | solution.py:30
  51.6 3.0 %convolution_convert_fusion = bf16[2,512,128]{1,2,0:T(8,128)(2,1)S(1)} fusion(bf16[512,2,128]{0,2,1:T(8,128)(2,1)} %bitcast.98, f32[2,512]{1,0:T(2,128)S(1)} %fusion.48, f32[2,512,512]{1,2,0:T(8,128)} %subtract_select_fusion), kind=kOutput, calls=%fused_computation.6 | convolution fusion | flops 135923200 | bytes 2625536 | tf_op jit(solution)/shard_map/hqk,khd->qhd/dot_general | solution.py:49
  54.6 0.9 constant_dynamic-slice_fusion.3
  55.7 0.7 slice.18
  56.4 0.8 pad_maximum_fusion.3
  57.2 0.8 fusion.9
  57.9 0.2 fusion.42
  58.2 0.2 fusion.27
  58.6 0.2 fusion.28
  58.9 0.9 constant_dynamic-slice_fusion.1
  59.8 0.1 copy.54
  60.1 0.7 slice.19
  60.8 0.8 pad_maximum_fusion.4
  61.8 0.1 copy.56
  61.9 0.8 pad_maximum_fusion
  62.8 0.6 broadcast_in_dim.20
  63.3 0.6 broadcast_in_dim.21
  64.1 0.9 copy.36
  65.0 75.5 %all-gather.2.cloned.1.call-done = bf16[514,2048]{0,1:T(8,128)(2,1)} async-done(((bf16[514,256]{0,1:T(8,128)(2,1)}), bf16[514,2048]{0,1:T(8,128)(2,1)}) %all-gather.2.cloned.1.call-update) | async-done | bytes 2105360 | tf_op jit(solution)/shard_map/all_gather | solution.py:135
  140.5 2.7 %fusion.53 = (f32[514]{0:T(1024)S(1)}, f32[514,256]{1,0:T(8,128)S(1)}) fusion(bf16[514,256]{1,0:T(8,128)(2,1)S(1)} %copy-done.8, f32[256]{0:T(256)S(1)} %copy-done.9, bf16[514,2048]{0,1:T(8,128)(2,1)} %all-gather.2.cloned.1.call-done, bf16[2048,256]{1,0:T(8,128)(2,1)S(1)} %copy-done), kind=kOutput, calls=%fused_computation.91 | convolution fusion | flops 539493888 | bytes 3946504 | tf_op jit(solution)/shard_map/dot_general | solution.py:134
  143.2 19.9 %psum.14 = f32[514]{0:T(1024)S(1)} all-reduce(f32[514]{0:T(1024)S(1)} %get-tuple-element.27), channel_id=1, replica_groups=mesh['rep'=64,'tp'=8] {'tp'}, use_global_device_ids=true, to_apply=%region_7.8 | all-reduce | flops 514 | bytes 4112 | tf_op jit(solution)/shard_map/psum | solution.py:142
  163.1 0.3 multiply_reduce_fusion
  163.3 21.8 %psum.15 = f32[514]{0:T(1024)S(1)} all-reduce(f32[514]{0:T(1024)S(1)} %multiply_reduce_fusion), channel_id=1, replica_groups=mesh['rep'=64,'tp'=8] {'tp'}, use_global_device_ids=true, to_apply=%region_9.10 | all-reduce | flops 514 | bytes 4112 | tf_op jit(solution)/shard_map/psum | solution.py:144
  185.1 1.0 add_convert_fusion
  (51 shorter events, 1.4 us)
Async XLA Ops:
  7.2 133.3 %copy-start = (bf16[2048,256]{1,0:T(8,128)(2,1)S(1)}, bf16[2048,256]{1,0:T(8,128)(2,1)}, u32[]{:S(2)}) copy-start(bf16[2048,256]{1,0:T(8,128)(2,1)} %param.27) | copy-start | bytes 3145732
  7.2 21.1 %copy-start.3 = (bf16[2,256]{1,0:T(2,128)(2,1)S(1)}, bf16[2,256]{1,0:T(2,128)(2,1)}, u32[]{:S(2)}) copy-start(bf16[2,256]{1,0:T(2,128)(2,1)} %param.24) | copy-start | bytes 3076
  7.2 25.8 %copy-start.5 = (s32[128]{0:T(128)S(1)}, s32[128]{0:T(128)}, u32[]{:S(2)}) copy-start(s32[128]{0:T(128)} %param.25) | copy-start | bytes 1540
  7.2 133.3 %all-gather.2.cloned.1.call-start = ((), (), s32[]{:S(2)}) async-start(), calls=%async_computation | async-start | bytes 2949120 | tf_op jit(solution)/shard_map/all_gather | solution.py:135
  10.5 29.0 %copy-start.2 = (bf16[2,256]{1,0:T(2,128)(2,1)S(1)}, bf16[2,256]{1,0:T(2,128)(2,1)}, u32[]{:S(2)}) copy-start(bf16[2,256]{1,0:T(2,128)(2,1)} %param.22) | copy-start | bytes 3076
  11.6 42.9 %collective-permute-start.1 = (bf16[1024,256]{1,0:T(8,128)(2,1)S(1)}, bf16[1024,256]{1,0:T(8,128)(2,1)}, u32[]{:S(2)}, u32[]{:S(2)}) collective-permute-start(bf16[1024,256]{1,0:T(8,128)(2,1)S(1)} %dynamic-slice_bitcast_fusion.1), channel_id=1, source_target_pairs={{256,0},{264,8},{272,16},{280,24},{288,32},{296,40},{304,48},{312,... | collective-permute-start | bytes 1572872 | tf_op jit(solution)/shard_map/ppermute | solution.py:19
  17.7 38.7 %collective-permute-start.2 = (bf16[256]{0:T(256)(128)(2,1)}, bf16[256]{0:T(256)(128)(2,1)}, u32[]{:S(2)}, u32[]{:S(2)}) collective-permute-start(bf16[256]{0:T(256)(128)(2,1)} %get-tuple-element.10), channel_id=1, source_target_pairs={{256,0},{264,8},{272,16},{280,24},{288,32},{296,40},{304,48},{312,... | collective-permute-start | bytes 1544 | tf_op jit(solution)/shard_map/ppermute | solution.py:19
  21.4 35.8 %collective-permute-start = (bf16[256]{0:T(256)(128)(2,1)}, bf16[256]{0:T(256)(128)(2,1)}, u32[]{:S(2)}, u32[]{:S(2)}) collective-permute-start(bf16[256]{0:T(256)(128)(2,1)} %fusion.35), channel_id=1, source_target_pairs={{256,0},{264,8},{272,16},{280,24},{288,32},{296,40},{304,48},{312,... | collective-permute-start | bytes 1544 | tf_op jit(solution)/shard_map/ppermute | solution.py:19
  25.9 33.0 %collective-permute-start.3 = (bf16[1024,256]{1,0:T(8,128)(2,1)S(1)}, bf16[1024,256]{1,0:T(8,128)(2,1)}, u32[]{:S(2)}, u32[]{:S(2)}) collective-permute-start(bf16[1024,256]{1,0:T(8,128)(2,1)S(1)} %dynamic-slice_bitcast_fusion), channel_id=1, source_target_pairs={{256,0},{264,8},{272,16},{280,24},{288,32},{296,40},{304,48},{312,... | collective-permute-start | bytes 1572872 | tf_op jit(solution)/shard_map/ppermute | solution.py:19
  28.9 31.9 %collective-permute-start.4 = (bf16[256]{0:T(256)(128)(2,1)}, bf16[256]{0:T(256)(128)(2,1)}, u32[]{:S(2)}, u32[]{:S(2)}) collective-permute-start(bf16[256]{0:T(256)(128)(2,1)} %get-tuple-element.12), channel_id=1, source_target_pairs={{256,0},{264,8},{272,16},{280,24},{288,32},{296,40},{304,48},{312,... | collective-permute-start | bytes 1544 | tf_op jit(solution)/shard_map/ppermute | solution.py:19
  46.5 3.0 %copy-start.4 = (f32[2]{0:T(128)S(1)}, f32[2]{0:T(128)}, u32[]{:S(2)}) copy-start(f32[2]{0:T(128)} %multiply_exponential_fusion) | copy-start | bytes 28
  51.6 6.9 %copy-start.1 = (bf16[260,2,128]{2,1,0:T(2,128)(2,1)S(1)}, bf16[260,2,128]{2,1,0:T(2,128)(2,1)}, u32[]{:S(2)}) copy-start(bf16[260,2,128]{2,1,0:T(2,128)(2,1)} %pad_maximum_fusion.2) | copy-start | bytes 399364
  57.2 83.3 %copy-start.8 = (bf16[514,256]{1,0:T(8,128)(2,1)S(1)}, bf16[514,256]{1,0:T(8,128)(2,1)}, u32[]{:S(2)}) copy-start(bf16[514,256]{1,0:T(8,128)(2,1)} %param.29) | copy-start | bytes 789508
  57.2 83.3 %copy-start.9 = (f32[256]{0:T(256)S(1)}, f32[256]{0:T(256)}, u32[]{:S(2)}) copy-start(f32[256]{0:T(256)} %param.28) | copy-start | bytes 3076
  65.0 120.1 %copy-start.6 = (f32[256]{0:T(256)S(1)}, f32[256]{0:T(256)}, u32[]{:S(2)}) copy-start(f32[256]{0:T(256)} %param.31) | copy-start | bytes 3076
  65.0 120.1 %copy-start.7 = (f32[256]{0:T(256)S(1)}, f32[256]{0:T(256)}, u32[]{:S(2)}) copy-start(f32[256]{0:T(256)} %param.30) | copy-start | bytes 3076
Sparse Core Ops, SparseCore 0:
  62.9 77.5 all-gather.1
where the time goes:
time: 194 us; the launch traced here: 193 us
  waiting for transfers between devices  75.5 us (39%)
  blocking collectives  41.6 us (21%)
  between operations  21.3 us (11%)
  local copies, waits for them, and re-layouts  17.8 us (9%)
  starting transfers between devices  15.1 us (8%)
  matrix products  11.9 us (6%)
  other arithmetic  9.62 us (5%)
    all_gather x1, waiting for transfers between devices, on_device(): lax.all_gather(mixed_rows, 'tp', axis=1, tiled=True)  75.5 us
    psum x1, blocking collectives, on_device(): row_var = lax.psum(jnp.sum(centered * centered, axis=1), 'tp') / D  21.8 us
    psum x1, blocking collectives, on_device(): row_mean = lax.psum(row_total, 'tp') / D  19.9 us
    ppermute x5, starting transfers between devices, from_behind(): return lax.ppermute(block, axis, route)  15.1 us
  transfers between devices with their start and end apart: 6, of which 1 were waited for; matrix products, arithmetic and copies ran while one was open for 16% of the time, Pallas kernels for 0%

commit v1 on v0

--- a/solution.py
+++ b/solution.py
@@ -132,7 +132,9 @@
     come_out = decode_attend(come_query, come_keys, come_values, come_len, slopes)
     mixed_rows = jnp.concatenate([prompt_mix, stay_out[None], come_out[None]], axis=0)
     projected = jnp.dot(
-        lax.all_gather(mixed_rows, "tp", axis=1, tiled=True),
+        jnp.concatenate(
+            lax.all_to_all(jnp.stack([mixed_rows] * lax.axis_size("tp")), "tp", 0, 0), axis=1
+        ),
         out_weight,
         preferred_element_type=jnp.float32,
     )

time: 194 us -> 139 us (0.72)
  the two profiles are of different devices: /device:TPU:32 before, /device:TPU:96 now
where the time goes in v1:
time: 139 us; the launch traced here: 138 us
  blocking collectives  41.7 us (30%)
  waiting for transfers between devices  25.2 us (18%)
  starting transfers between devices  21.8 us (16%)
  local copies, waits for them, and re-layouts  21.6 us (16%)
  other arithmetic  10.1 us (7%)
  matrix products  10.1 us (7%)
  between operations  7.96 us (6%)
    all_to_all x1, waiting for transfers between devices, on_device(): lax.all_to_all(jnp.stack([mixed_rows] * lax.axis_size('tp')), 'tp', 0, 0)  25.2 us
    psum x1, blocking collectives, on_device(): row_var = lax.psum(jnp.sum(centered * centered, axis=1), 'tp') / D  21.1 us
    psum x1, blocking collectives, on_device(): row_mean = lax.psum(row_total, 'tp') / D  20.5 us
    ppermute x5, starting transfers between devices, from_behind(): return lax.ppermute(block, axis, route)  15.2 us
    all_to_all x1, starting transfers between devices, on_device(): lax.all_to_all(jnp.stack([mixed_rows] * lax.axis_size('tp')), 'tp', 0, 0)  6.64 us
    dynamic_slice x3, local copies, waits for them, and re-layouts, select_slot(): return lax.dynamic_index_in_dim(stacked, slot_index, 0, keepdims=False)  3.85 us
    concatenate x4, other arithmetic, window_rows(): return jnp.concatenate([cache_rows[:SINK], middle, newest[None]], axis=0)  3.29 us
    dot_general x1, matrix products, prompt_attend(): jnp.einsum('hqk,khd->qhd', weights, value_heads, preferred_element_type=j...  3.01 us
  transfers between devices with their start and end apart: 6, of which 1 were waited for; matrix products, arithmetic and copies ran while one was open for 24% of the time, Pallas kernels for 0%

profile of v1, /device:TPU:96, one launch (start us, length us, event | category | flops | bytes accessed | tf_op | source)
XLA Modules:
  0.0 138.5 jit_solution(8724017512958162649)
XLA Ops:
  0.7 1.3 fusion.47
  5.3 1.3 fusion.33
  6.6 3.4 %collective-permute-start.2 = (bf16[256]{0:T(256)(128)(2,1)}, bf16[256]{0:T(256)(128)(2,1)}, u32[]{:S(2)}, u32[]{:S(2)}) collective-permute-start(bf16[256]{0:T(256)(128)(2,1)} %get-tuple-element.13), channel_id=1, source_target_pairs={{256,0},{264,8},{272,16},{280,24},{288,32},{296,40},{304,48},{312,... | collective-permute-start | bytes 1544 | tf_op jit(solution)/shard_map/ppermute | solution.py:19
  10.0 1.4 fusion.34
  11.3 2.4 %collective-permute-start.4 = (bf16[256]{0:T(256)(128)(2,1)}, bf16[256]{0:T(256)(128)(2,1)}, u32[]{:S(2)}, u32[]{:S(2)}) collective-permute-start(bf16[256]{0:T(256)(128)(2,1)} %get-tuple-element.15), channel_id=1, source_target_pairs={{256,0},{264,8},{272,16},{280,24},{288,32},{296,40},{304,48},{312,... | collective-permute-start | bytes 1544 | tf_op jit(solution)/shard_map/ppermute | solution.py:19
  13.8 1.2 fusion.35
  15.0 3.5 %collective-permute-start = (bf16[256]{0:T(256)(128)(2,1)}, bf16[256]{0:T(256)(128)(2,1)}, u32[]{:S(2)}, u32[]{:S(2)}) collective-permute-start(bf16[256]{0:T(256)(128)(2,1)} %fusion.35), channel_id=1, source_target_pairs={{256,0},{264,8},{272,16},{280,24},{288,32},{296,40},{304,48},{312,... | collective-permute-start | bytes 1544 | tf_op jit(solution)/shard_map/ppermute | solution.py:19
  18.5 1.1 dynamic-slice_bitcast_fusion.1
  19.6 2.4 %collective-permute-start.1 = (bf16[1024,256]{1,0:T(8,128)(2,1)S(1)}, bf16[1024,256]{1,0:T(8,128)(2,1)}, u32[]{:S(2)}, u32[]{:S(2)}) collective-permute-start(bf16[1024,256]{1,0:T(8,128)(2,1)S(1)} %dynamic-slice_bitcast_fusion.1), channel_id=1, source_target_pairs={{256,0},{264,8},{272,16},{280,24},{288,32},{296,40},{304,48},{312,... | collective-permute-start | bytes 1572872 | tf_op jit(solution)/shard_map/ppermute | solution.py:19
  22.0 1.1 dynamic-slice_bitcast_fusion
  23.1 3.4 %collective-permute-start.3 = (bf16[1024,256]{1,0:T(8,128)(2,1)S(1)}, bf16[1024,256]{1,0:T(8,128)(2,1)}, u32[]{:S(2)}, u32[]{:S(2)}) collective-permute-start(bf16[1024,256]{1,0:T(8,128)(2,1)S(1)} %dynamic-slice_bitcast_fusion), channel_id=1, source_target_pairs={{256,0},{264,8},{272,16},{280,24},{288,32},{296,40},{304,48},{312,... | collective-permute-start | bytes 1572872 | tf_op jit(solution)/shard_map/ppermute | solution.py:19
  27.2 0.6 fusion.46
  30.2 0.6 iota_add_fusion
  30.8 0.7 constant_dynamic-slice_fusion.7
  31.5 0.7 constant_dynamic-slice_fusion.10
  33.0 0.6 multiply_exponential_fusion
  33.5 0.6 iota_compare_fusion.1
  34.1 1.0 constant_dynamic-slice_fusion.6
  35.8 0.8 fusion.2
  36.6 1.8 %copy.63 = bf16[512,256]{0,1:T(8,128)(2,1)} copy(bf16[512,256]{1,0:T(8,128)(2,1)} %param.18) | data formatting | bytes 524288 | tf_op jit(solution)/shard_map/reshape | solution.py:39
  38.4 2.0 %fusion.24 = (f32[260]{0:T(512)S(1)}, f32[260]{0:T(512)S(1)}) fusion(s32[4]{0:T(128)S(1)} %iota.55, s32[256]{0:T(256)} %get-tuple-element.33, s32[]{:T(128)} %bitcast.6, s32[256]{0:T(256)} %get-tuple-element.32, s32[]{:T(128)} %bitcast.15), kind=kLoop, calls=%fused_computation.60 | loop fusion | flops 1560 | bytes 4152 | tf_op jit(solution)/shard_map/convert_element_type | solution.py:74
  40.4 1.5 %pad_maximum_fusion.2 = bf16[260,2,128]{2,1,0:T(2,128)(2,1)} fusion(bf16[1,2,128]{2,1,0:T(2,128)(2,1)} %bitcast.107, bf16[255,2,128]{2,1,0:T(2,128)(2,1)S(1)} %concatenate.67, bf16[4,2,128]{2,1,0:T(2,128)(2,1)S(1)} %concatenate.66), kind=kLoop, calls=%fused_computation.31 | loop fusion | flops 133120 | bytes 266240 | tf_op jit(solution)/shard_map/concatenate | solution.py:57
  41.9 3.0 %subtract_select_fusion = f32[2,512,512]{1,2,0:T(8,128)} fusion(f32[512,512]{0,1:T(8,128)S(1)} %subtract_convert_fusion, f32[2]{0:T(128)} %multiply_exponential_fusion, pred[512,512]{0,1:T(8,128)(4,1)S(1)} %fusion.2, bf16[512,256]{1,0:T(8,128)(2,1)} %param.17, bf16[512,256]{1,0:T(8,128)(2,1)} %param.16), kind=kOutput, calls=%fused_computation.3 | convolution fusion | flops 136314880 | bytes 3932168 | tf_op jit(solution)/shard_map/qhd,khd->hqk/dot_general | solution.py:40
  44.9 2.0 %fusion.48 = f32[2,512]{1,0:T(2,128)S(1)} fusion(f32[512,512]{0,1:T(8,128)S(1)} %subtract_convert_fusion, f32[2]{0:T(128)S(1)} %copy-done.3, pred[512,512]{0,1:T(8,128)(4,1)S(1)} %fusion.2, bf16[512,256]{1,0:T(8,128)(2,1)} %param.17, bf16[512,256]{1,0:T(8,128)(2,1)} %param.16), kind=kOutput, calls=%fused_computation.90 | convolution fusion | flops 137363968 | bytes 1839112 | tf_op jit(solution)/shard_map/sub | solution.py:30
  47.0 3.0 %convolution_convert_fusion = bf16[2,512,128]{1,2,0:T(8,128)(2,1)S(1)} fusion(bf16[512,2,128]{0,2,1:T(8,128)(2,1)} %bitcast.105, f32[2,512]{1,0:T(2,128)S(1)} %fusion.48, f32[2,512,512]{1,2,0:T(8,128)} %subtract_select_fusion), kind=kOutput, calls=%fused_computation.6 | convolution fusion | flops 135923200 | bytes 2625536 | tf_op jit(solution)/shard_map/hqk,khd->qhd/dot_general | solution.py:49
  50.0 0.9 constant_dynamic-slice_fusion.3
  50.9 0.7 slice.18
  51.8 0.8 pad_maximum_fusion.3
  52.6 0.8 fusion.9
  53.4 0.2 fusion.42
  54.0 0.2 fusion.28
  54.3 0.9 constant_dynamic-slice_fusion.1
  55.4 0.7 slice.19
  56.2 0.8 pad_maximum_fusion.4
  57.6 1.5 %stack.8 = bf16[8,514,256]{2,1,0:T(8,128)(2,1)} broadcast(bf16[514,256]{1,0:T(8,128)(2,1)S(1)} %copy.47), dimensions={1,2} | broadcast | bytes 2368512 | tf_op jit(solution)/shard_map/stack | solution.py:136
  59.1 6.6 %all-to-all-start = ((bf16[8,514,256]{2,1,0:T(8,128)(2,1)}), bf16[8,514,256]{2,1,0:T(8,128)(2,1)S(1)}, u32[]{:S(2)}, u32[]{:S(2)}) async-start(bf16[8,514,256]{2,1,0:T(8,128)(2,1)} %stack.8), calls=%async_computation | async-start | bytes 4259840 | tf_op jit(solution)/shard_map/all_to_all | solution.py:136
  65.7 0.6 broadcast_in_dim.20
  66.3 0.6 broadcast_in_dim.21
  67.0 0.9 copy.49
  68.0 25.2 %all-to-all-done = bf16[8,514,256]{2,1,0:T(8,128)(2,1)S(1)} async-done(((bf16[8,514,256]{2,1,0:T(8,128)(2,1)}), bf16[8,514,256]{2,1,0:T(8,128)(2,1)S(1)}, u32[]{:S(2)}, u32[]{:S(2)}) %all-to-all-start) | async-done | bytes 2105376 | tf_op jit(solution)/shard_map/all_to_all | solution.py:136
  93.1 0.4 copy.48
  93.7 0.7 copy.70
  94.4 0.2 copy-done.7
  94.7 0.9 fusion.53
  95.5 20.5 %psum.14 = f32[514]{0:T(1024)S(1)} all-reduce(f32[514]{0:T(1024)S(1)} %get-tuple-element.30), channel_id=1, replica_groups=mesh['rep'=64,'tp'=8] {'tp'}, use_global_device_ids=true, to_apply=%region_7.8 | all-reduce | flops 514 | bytes 4112 | tf_op jit(solution)/shard_map/psum | solution.py:144
  116.1 0.3 multiply_reduce_fusion
  116.4 21.1 %psum.15 = f32[514]{0:T(1024)S(1)} all-reduce(f32[514]{0:T(1024)S(1)} %multiply_reduce_fusion), channel_id=1, replica_groups=mesh['rep'=64,'tp'=8] {'tp'}, use_global_device_ids=true, to_apply=%region_9.10 | all-reduce | flops 514 | bytes 4112 | tf_op jit(solution)/shard_map/psum | solution.py:146
  137.5 1.0 add_convert_fusion
  (53 shorter events, 2.5 us)
Async XLA Ops:
  0.6 93.8 %copy-start = (bf16[2048,256]{1,0:T(8,128)(2,1)S(1)}, bf16[2048,256]{1,0:T(8,128)(2,1)}, u32[]{:S(2)}) copy-start(bf16[2048,256]{1,0:T(8,128)(2,1)} %param.27) | copy-start | bytes 3145732
  0.6 26.5 %copy-start.4 = (s32[128]{0:T(128)S(1)}, s32[128]{0:T(128)}, u32[]{:S(2)}) copy-start(s32[128]{0:T(128)} %param.25) | copy-start | bytes 1540
  6.6 45.2 %collective-permute-start.2 = (bf16[256]{0:T(256)(128)(2,1)}, bf16[256]{0:T(256)(128)(2,1)}, u32[]{:S(2)}, u32[]{:S(2)}) collective-permute-start(bf16[256]{0:T(256)(128)(2,1)} %get-tuple-element.13), channel_id=1, source_target_pairs={{256,0},{264,8},{272,16},{280,24},{288,32},{296,40},{304,48},{312,... | collective-permute-start | bytes 1544 | tf_op jit(solution)/shard_map/ppermute | solution.py:19
  11.3 44.9 %collective-permute-start.4 = (bf16[256]{0:T(256)(128)(2,1)}, bf16[256]{0:T(256)(128)(2,1)}, u32[]{:S(2)}, u32[]{:S(2)}) collective-permute-start(bf16[256]{0:T(256)(128)(2,1)} %get-tuple-element.15), channel_id=1, source_target_pairs={{256,0},{264,8},{272,16},{280,24},{288,32},{296,40},{304,48},{312,... | collective-permute-start | bytes 1544 | tf_op jit(solution)/shard_map/ppermute | solution.py:19
  15.0 20.7 %copy-start.2 = (bf16[2,256]{1,0:T(2,128)(2,1)S(1)}, bf16[2,256]{1,0:T(2,128)(2,1)}, u32[]{:S(2)}) copy-start(bf16[2,256]{1,0:T(2,128)(2,1)} %param.22) | copy-start | bytes 3076
  15.0 37.6 %collective-permute-start = (bf16[256]{0:T(256)(128)(2,1)}, bf16[256]{0:T(256)(128)(2,1)}, u32[]{:S(2)}, u32[]{:S(2)}) collective-permute-start(bf16[256]{0:T(256)(128)(2,1)} %fusion.35), channel_id=1, source_target_pairs={{256,0},{264,8},{272,16},{280,24},{288,32},{296,40},{304,48},{312,... | collective-permute-start | bytes 1544 | tf_op jit(solution)/shard_map/ppermute | solution.py:19
  19.6 30.4 %collective-permute-start.1 = (bf16[1024,256]{1,0:T(8,128)(2,1)S(1)}, bf16[1024,256]{1,0:T(8,128)(2,1)}, u32[]{:S(2)}, u32[]{:S(2)}) collective-permute-start(bf16[1024,256]{1,0:T(8,128)(2,1)S(1)} %dynamic-slice_bitcast_fusion.1), channel_id=1, source_target_pairs={{256,0},{264,8},{272,16},{280,24},{288,32},{296,40},{304,48},{312,... | collective-permute-start | bytes 1572872 | tf_op jit(solution)/shard_map/ppermute | solution.py:19
  23.1 31.2 %collective-permute-start.3 = (bf16[1024,256]{1,0:T(8,128)(2,1)S(1)}, bf16[1024,256]{1,0:T(8,128)(2,1)}, u32[]{:S(2)}, u32[]{:S(2)}) collective-permute-start(bf16[1024,256]{1,0:T(8,128)(2,1)S(1)} %dynamic-slice_bitcast_fusion), channel_id=1, source_target_pairs={{256,0},{264,8},{272,16},{280,24},{288,32},{296,40},{304,48},{312,... | collective-permute-start | bytes 1572872 | tf_op jit(solution)/shard_map/ppermute | solution.py:19
  41.9 3.0 %copy-start.3 = (f32[2]{0:T(128)S(1)}, f32[2]{0:T(128)}, u32[]{:S(2)}) copy-start(f32[2]{0:T(128)} %multiply_exponential_fusion) | copy-start | bytes 28
  47.0 6.9 %copy-start.1 = (bf16[260,2,128]{2,1,0:T(2,128)(2,1)S(1)}, bf16[260,2,128]{2,1,0:T(2,128)(2,1)}, u32[]{:S(2)}) copy-start(bf16[260,2,128]{2,1,0:T(2,128)(2,1)} %pad_maximum_fusion.2) | copy-start | bytes 399364
  59.1 34.0 %all-to-all-start = ((bf16[8,514,256]{2,1,0:T(8,128)(2,1)}), bf16[8,514,256]{2,1,0:T(8,128)(2,1)S(1)}, u32[]{:S(2)}, u32[]{:S(2)}) async-start(bf16[8,514,256]{2,1,0:T(8,128)(2,1)} %stack.8), calls=%async_computation | async-start | bytes 4259840 | tf_op jit(solution)/shard_map/all_to_all | solution.py:136
  93.7 1.0 copy-start.7
  93.7 0.9 copy-start.8
  94.7 42.8 %copy-start.5 = (f32[256]{0:T(256)S(1)}, f32[256]{0:T(256)}, u32[]{:S(2)}) copy-start(f32[256]{0:T(256)} %param.31) | copy-start | bytes 3076
  94.7 42.8 %copy-start.6 = (f32[256]{0:T(256)S(1)}, f32[256]{0:T(256)}, u32[]{:S(2)}) copy-start(f32[256]{0:T(256)} %param.30) | copy-start | bytes 3076
